TPU v7x, 768 devices: a whole 4x8x12 slice. The times are simulated.
768 devices in a mesh: dp: 24 (over z_lo, x, core), mp: 32 (over z_hi, y).
Axes of the slice: x: 4, y: 8, z: 12 (z_hi: 4, z_lo: 3; z = z_hi * 3 + z_lo), core: 2. Of those that a mesh axis runs over, the one named last changes fastest.
Arguments:
- prelude_output: bfloat16 [72, 32, 5280], P('dp', None, 'mp'), may hold values from -6 to 6
- init_noise: bfloat16 [96, 32, 5280], P('dp', None, 'mp'), may hold values from -6 to 6
- core_weight: bfloat16 [5280, 5280], P('mp'), may hold values from -0.078125 to 0.078125
- norm_gain: float32 [5280], replicated, may hold values from 0.5 to 1.5
- state_cotangent: bfloat16 [96, 32, 5280], P('dp', None, 'mp'), may hold values from -6 to 6
- step_counts: int32 [72], replicated, may hold values from 1 to 3, as said below
- group_table: int32 [72], replicated, may hold values from 0 to 23, as said below
Outputs:
- weight_grad: float32 [5280, 5280], P('mp', 'dp')
Inputs may be any that keep to these rules, and one draw needn't show every extreme that they name: `step_counts`: sequences in the groups that run fewer sequences all take 3 steps. `group_table`: half of the groups run 4 sequences and the other half run 2 (their other 2 slots stay empty).
All inputs are finite; a program needn't handle non-finite values.
Results may differ from a plain program's by a relative error of at most 0.025.
Values may be sent and summed in bfloat16 or wider, within the bound.
No kernel may reach another device: no remote copies, remote signals or barrier semaphores. Data moves between devices by JAX's collectives and lax.ppermute only.
A program may use at most 32 MiB of HBM per device.

v0:
```python
import jax
import jax.numpy as jnp
from jax import lax
from jax.sharding import PartitionSpec as P

MAXR = 3
BP = 2


EPS = 1e-06


def local(
    prelude_output, init_noise, core_weight, norm_gain, state_cotangent, step_counts, group_table
):
    full_width = core_weight.shape[1]
    local_width = core_weight.shape[0]
    slot_total = init_noise.shape[0]
    seq_length = init_noise.shape[1]
    row_count = slot_total * seq_length
    my_group = lax.axis_index("dp")
    column_first = lax.axis_index("mp") * local_width
    seq_total = group_table.shape[0]
    seq_index = jnp.arange(seq_total, dtype=jnp.int32)
    earlier = (group_table[:, None] == group_table[None, :]) & (
        seq_index[None, :] < seq_index[:, None]
    )
    slot_rank = jnp.sum(earlier.astype(jnp.int32), axis=1)
    selected_rows = (group_table[None, :] == my_group) & (
        slot_rank[None, :] == jnp.arange(slot_total, dtype=jnp.int32)[:, None]
    )
    slot_counts = jnp.sum(jnp.where(selected_rows, step_counts[None, :], 0), axis=1)
    chosen_weights = selected_rows.astype(jnp.bfloat16)
    injected_input = jnp.einsum(
        "br,ref->bef",
        chosen_weights,
        lax.all_gather(prelude_output, "dp", axis=0, tiled=True),
        preferred_element_type=jnp.float32,
    ).reshape(row_count, local_width)
    gain_local = lax.dynamic_slice_in_dim(norm_gain, column_first, local_width, 0)

    def feature_sum(values):
        return lax.psum(values, "mp")

    shard_state = init_noise.reshape(row_count, local_width)
    saved = []
    for turn in range(MAXR):
        active = jnp.repeat(turn >= MAXR - slot_counts, seq_length)[:, None]
        piece_rows = lax.all_gather(shard_state, "mp", axis=1, tiled=True)
        product = lax.dot_general(
            piece_rows, core_weight, (((1,), (1,)), ((), ())), preferred_element_type=jnp.float32
        )
        whole_state = piece_rows
        product, whole_state = (product, whole_state)
        mixed = (product + injected_input).astype(jnp.bfloat16)
        mixed_float = mixed.astype(jnp.float32)
        inverse_rms = lax.rsqrt(
            feature_sum(jnp.sum(mixed_float * mixed_float, axis=1)) / full_width + EPS
        )
        renewed = (gain_local * mixed_float * inverse_rms[:, None]).astype(jnp.bfloat16)
        saved.append((whole_state, mixed_float, inverse_rms, active))
        shard_state = jnp.where(active, renewed, shard_state)
    upstream = state_cotangent.reshape(row_count, local_width).astype(jnp.float32)
    weight_grad = jnp.zeros((local_width, full_width), jnp.float32)
    for back_index in range(BP):
        whole_state, mixed_float, inverse_rms, active = saved[MAXR - 1 - back_index]
        scaled = upstream * gain_local
        inner = feature_sum(jnp.sum(scaled * mixed_float, axis=1))
        delta = (
            inverse_rms[:, None] * scaled
            - mixed_float * (inverse_rms**3 * inner / full_width)[:, None]
        )
        delta_b = jnp.where(active, delta, 0.0).astype(jnp.bfloat16)
        weight_grad = weight_grad + lax.dot_general(
            delta_b, whole_state, (((0,), (0,)), ((), ())), preferred_element_type=jnp.float32
        )
        if back_index + 1 < BP:
            partial_rows = jnp.dot(delta_b, core_weight, preferred_element_type=jnp.float32)
            summed_rows = lax.psum_scatter(
                partial_rows.astype(jnp.bfloat16), "mp", scatter_dimension=1, tiled=True
            ).astype(jnp.float32)
            upstream = jnp.where(active, summed_rows, upstream)
    return lax.psum_scatter(
        weight_grad.astype(jnp.bfloat16), "dp", scatter_dimension=1, tiled=True
    ).astype(jnp.float32)


def solution(mesh):
    return jax.shard_map(
        local,
        mesh=mesh,
        in_specs=(
            P("dp", None, "mp"),
            P("dp", None, "mp"),
            P("mp", None),
            P(),
            P("dp", None, "mp"),
            P(),
            P(),
        ),
        out_specs=P("mp", "dp"),
        check_vma=False,
    )
```

profile of v0, /device:TPU:192, one launch (start us, length us, event | category | flops | bytes accessed | tf_op | source)
XLA Modules:
  0.0 1003.6 jit_solution(18223811297982269851)
XLA Ops:
  6.5 1.7 copy.30
  8.3 0.9 convert_reduce_fusion
  9.2 0.7 broadcast_compare_fusion.3
  9.9 0.8 select_reduce_fusion
  10.7 0.1 broadcast_in_dim.88
  10.8 0.1 broadcast_in_dim.89
  10.8 0.9 copy.34
  11.8 40.9 %all_gather.13 = bf16[72,32,165]{2,1,0:T(8,128)(2,1)S(1)} all-gather(bf16[3,32,165]{2,1,0:T(8,128)(2,1)} %param.7), channel_id=1, replica_groups=mesh['dp'=24,'mp'=32] {'dp'}, dimensions={0}, use_global_device_ids=true | all-gather | bytes 792000 | tf_op jit(solution)/shard_map/all_gather | solution.py:37
  52.7 0.8 fusion.2
  53.5 0.1 copy.33
  53.6 0.8 dynamic_slice.3
  54.4 54.3 %all-gather.7.cloned.1.call-done = bf16[32,165,128]{2,1,0:T(8,128)(2,1)} async-done(((bf16[1,165,128]{2,1,0:T(8,128)(2,1)}), bf16[32,165,128]{2,1,0:T(8,128)(2,1)}) %all-gather.7.cloned.1.call-update) | async-done | bytes 1351696 | tf_op jit(solution)/shard_map/all_gather | solution.py:49
  108.8 1.5 reshape.28
  110.3 0.7 multiply_reduce_fusion.4
  111.0 79.5 %psum.35 = f32[128]{0:T(128)S(1)} all-reduce(f32[128]{0:T(128)S(1)} %get-tuple-element.14), channel_id=1, replica_groups=mesh['dp'=24,'mp'=32] {'mp'}, use_global_device_ids=true, to_apply=%region_3.4 | all-reduce | flops 128 | bytes 1024 | tf_op jit(solution)/shard_map/psum | solution.py:43
  190.5 0.7 fusion.10
  191.3 0.1 broadcast_in_dim.85
  191.4 0.1 broadcast_in_dim.86
  191.5 95.2 %all-gather.9.cloned.1.call-done = bf16[32,165,128]{2,1,0:T(8,128)(2,1)} async-done(((bf16[1,165,128]{2,1,0:T(8,128)(2,1)}), bf16[32,165,128]{2,1,0:T(8,128)(2,1)}) %all-gather.9.cloned.1.call-update) | async-done | bytes 1351696 | tf_op jit(solution)/shard_map/all_gather | solution.py:49
  286.7 1.5 reshape.30
  288.2 0.7 multiply_reduce_fusion.3
  288.9 79.5 %psum.36 = f32[128]{0:T(128)S(1)} all-reduce(f32[128]{0:T(128)S(1)} %get-tuple-element.16), channel_id=1, replica_groups=mesh['dp'=24,'mp'=32] {'mp'}, use_global_device_ids=true, to_apply=%region_5.6 | all-reduce | flops 128 | bytes 1024 | tf_op jit(solution)/shard_map/psum | solution.py:43
  368.5 0.7 fusion.12
  369.2 0.0 all-reduce.6.cloned.1.call-start
  369.2 0.1 broadcast_in_dim.82
  369.3 0.1 broadcast_in_dim.83
  369.4 0.9 bitcast_convert_fusion
  370.3 0.1 copy.37
  370.4 1.3 dynamic-slice.6
  372.3 92.2 %all-gather.11.cloned.1.call-done = bf16[32,165,128]{2,1,0:T(8,128)(2,1)} async-done(((bf16[1,165,128]{2,1,0:T(8,128)(2,1)}), bf16[32,165,128]{2,1,0:T(8,128)(2,1)}) %all-gather.11.cloned.1.call-update) | async-done | bytes 1351696 | tf_op jit(solution)/shard_map/all_gather | solution.py:49
  464.5 2.4 reshape.32
  466.9 2.0 multiply_reduce_fusion.2
  468.9 79.6 %all-reduce.3 = (f32[128]{0:T(128)S(1)}, f32[128]{0:T(128)S(1)}) all-reduce(f32[128]{0:T(128)S(1)} %get-tuple-element.6, f32[128]{0:T(128)S(1)} %get-tuple-element.5), channel_id=1, replica_groups=mesh['dp'=24,'mp'=32] {'mp'}, use_global_device_ids=true, to_apply=%region_9.10 | all-reduce | flops 256 | bytes 2048 | tf_op jit(solution)/shard_map/psum | solution.py:43
  548.6 0.1 select_convert_fusion.1
  548.7 2.3 convolution_convert_fusion
  550.9 90.9 %fusion = bf16[128,176]{0,1:T(8,128)(2,1)S(1)} fusion(bf16[128,5280]{0,1:T(8,128)(2,1)} %convolution_convert_fusion), kind=kCustom, calls=%all-reduce-scatter | all-reduce-scatter fusion | flops 720897 | bytes 1400832
  641.9 4.1 collective-permute-start
  646.0 3.6 collective-permute-start.1
  649.6 4.2 fusion.32
  653.7 3.0 collective-permute-done.1
  656.7 0.6 copy-done.2
  657.4 2.0 concatenate
  659.4 0.1 multiply_reduce_fusion
  659.5 81.9 %psum.39 = f32[128]{0:T(128)S(1)} all-reduce(f32[128]{0:T(128)S(1)} %multiply_reduce_fusion), channel_id=1, replica_groups=mesh['dp'=24,'mp'=32] {'mp'}, use_global_device_ids=true, to_apply=%region_12.13 | all-reduce | flops 128 | bytes 1024 | tf_op jit(solution)/shard_map/psum | solution.py:43
  741.4 4.3 fusion.1
  745.8 1.3 dynamic-slice.2
  747.7 247.7 %all-reduce.6.cloned.1.call-done = bf16[165,5280]{1,0:T(8,128)(2,1)} async-done(((bf16[165,5280]{1,0:T(8,128)(2,1)}), bf16[165,5280]{1,0:T(8,128)(2,1)}) %all-reduce.6.cloned.1.call-update) | async-done | bytes 1742416
  995.4 1.7 dynamic-slice_convert_fusion
  (36 shorter events, 0.3 us)
Async XLA Ops:
  6.5 103.8 %copy-start = (bf16[165,5280]{1,0:T(8,128)(2,1)S(1)}, bf16[165,5280]{1,0:T(8,128)(2,1)}, u32[]{:S(2)}) copy-start(bf16[165,5280]{1,0:T(8,128)(2,1)} %param.9) | copy-start | bytes 5227204
  6.5 102.2 %all-gather.7.cloned.1.call-start = ((), (), s32[]{:S(2)}) async-start(), calls=%async_computation | async-start | bytes 1419264 | tf_op jit(solution)/shard_map/all_gather | solution.py:49
  8.3 278.4 %all-gather.9.cloned.1.call-start = ((), (), s32[]{:S(2)}) async-start(), calls=%async_computation.1 | async-start | bytes 1419264 | tf_op jit(solution)/shard_map/all_gather | solution.py:49
  191.3 273.2 %all-gather.11.cloned.1.call-start = ((), (), s32[]{:S(2)}) async-start(), calls=%async_computation.2 | async-start | bytes 1419264 | tf_op jit(solution)/shard_map/all_gather | solution.py:49
  191.5 177.0 %copy-start.5 = (pred[128]{0:T(512)(128)(4,1)}, pred[128]{0:T(512)(128)(4,1)S(1)}, u32[]{:S(2)}) copy-start(pred[128]{0:T(512)(128)(4,1)S(1)} %broadcast_in_dim.86) | copy-start | bytes 388
  288.2 80.2 %copy-start.1 = (bf16[128,165]{0,1:T(8,128)(2,1)S(1)}, bf16[128,165]{0,1:T(8,128)(2,1)}, u32[]{:S(2)}) copy-start(bf16[128,165]{0,1:T(8,128)(2,1)} %fusion.10) | copy-start | bytes 126724
  368.4 1.0 copy-start.9
  368.4 1.0 copy-start.7
  369.2 626.2 %all-reduce.6.cloned.1.call-start = ((), (), s32[]{:S(2)}) async-start(), calls=%async_computation.3 | async-start | bytes 3612672
  369.4 179.1 %copy-start.3 = (pred[128]{0:T(512)(128)(4,1)}, pred[128]{0:T(512)(128)(4,1)S(1)}, u32[]{:S(2)}) copy-start(pred[128]{0:T(512)(128)(4,1)S(1)} %broadcast_in_dim.83) | copy-start | bytes 388
  641.9 17.5 %copy-start.4 = (pred[128]{0:T(512)(128)(4,1)S(1)}, pred[128]{0:T(512)(128)(4,1)}, u32[]{:S(2)}) copy-start(pred[128]{0:T(512)(128)(4,1)} %copy-done.3) | copy-start | bytes 388
  641.9 99.5 %copy-start.10 = (f32[128]{0:T(128)S(1)}, f32[128]{0:T(128)}, u32[]{:S(2)}) copy-start(f32[128]{0:T(128)} %copy-done.9) | copy-start | bytes 1540
  641.9 99.5 %copy-start.6 = (pred[128]{0:T(512)(128)(4,1)S(1)}, pred[128]{0:T(512)(128)(4,1)}, u32[]{:S(2)}) copy-start(pred[128]{0:T(512)(128)(4,1)} %copy-done.5) | copy-start | bytes 388
  641.9 99.5 %copy-start.8 = (f32[128]{0:T(128)S(1)}, f32[128]{0:T(128)}, u32[]{:S(2)}) copy-start(f32[128]{0:T(128)} %copy-done.7) | copy-start | bytes 1540
  641.9 15.4 %collective-permute-start = (bf16[128,176]{0,1:T(8,128)(2,1)S(1)}, bf16[128,176]{0,1:T(8,128)(2,1)}, u32[]{:S(2)}, u32[]{:S(2)}) collective-permute-start(bf16[128,176]{0,1:T(8,128)(2,1)S(1)} %fusion), channel_id=1, source_target_pairs={{0,1},{1,2},{2,3},{3,4},{4,5},{5,6},{6,7},{7,8},{8,9},{9,10},{10,1... | collective-permute-start | bytes 135176
  646.0 10.7 %collective-permute-start.1 = (bf16[128,165]{0,1:T(8,128)(2,1)S(1)}, bf16[128,165]{0,1:T(8,128)(2,1)S(1)}, u32[]{:S(2)}, u32[]{:S(2)}) collective-permute-start(bf16[128,165]{0,1:T(8,128)(2,1)S(1)} %slice), channel_id=1, source_target_pairs={{0,2},{1,3},{2,4},{3,5},{4,6},{5,7},{6,8},{7,9},{8,10},{9,11},{10,... | collective-permute-start | bytes 126728
  656.7 0.6 copy-start.2
Sparse Core Ops, SparseCore 0:
  11.0 97.6 all-gather.6
  191.4 95.2 all-gather.8
  369.3 95.1 all-gather.10
  745.9 249.4 all-reduce.5
where the time goes:
time: 1000 us
  waiting for transfers between devices  492 us (49%)
  blocking collectives  452 us (45%)
  matrix products  15 us (2%)
  local copies, waits for them, and re-layouts  14.8 us (1%)
  between operations  14.7 us (1%)
    psum x4, blocking collectives, feature_sum(): return lax.psum(values, 'mp')  320 us
    unnamed x7, waiting for transfers between devices  251 us
    all_gather x3, waiting for transfers between devices, local(): piece_rows = lax.all_gather(shard_state, 'mp', axis=1, tiled=True)  242 us
    unnamed x1, blocking collectives  90.9 us
    all_gather x1, blocking collectives, local(): lax.all_gather(prelude_output, 'dp', axis=0, tiled=True)  40.9 us
  transfers between devices with their start and end apart: 6, of which 5 were waited for; matrix products, arithmetic and copies ran while one was open for 1% of the time, Pallas kernels for 0%

commit v1 on v0

v1 whole, which is shorter than its diff:
```python
import jax
import jax.numpy as jnp
from jax import lax
from jax.sharding import PartitionSpec as P

MAXR = 3
EPS = 1e-06


def spread(block, axis, count):
    return lax.all_to_all(jnp.broadcast_to(block[None], (count,) + block.shape), axis, 0, 0)


def local(
    prelude_output, init_noise, core_weight, norm_gain, state_cotangent, step_counts, group_table
):
    local_width, full_width = core_weight.shape
    slot_total, seq_length = init_noise.shape[:2]
    rows = slot_total * seq_length
    mp_count = full_width // local_width
    dp_count = lax.axis_size("dp")
    my_group = lax.axis_index("dp")
    column_first = lax.axis_index("mp") * local_width
    seq_index = jnp.arange(group_table.shape[0], dtype=jnp.int32)

    noise = init_noise.reshape(rows, local_width).T
    first_state = spread(noise, "mp", mp_count).reshape(full_width, rows)

    earlier = (group_table[:, None] == group_table[None, :]) & (
        seq_index[None, :] < seq_index[:, None]
    )
    slot_rank = jnp.sum(earlier.astype(jnp.int32), axis=1)
    selected = (group_table[None, :] == my_group) & (
        slot_rank[None, :] == jnp.arange(slot_total, dtype=jnp.int32)[:, None]
    )
    slot_counts = jnp.sum(jnp.where(selected, step_counts[None, :], 0), axis=1)
    token_counts = jnp.repeat(slot_counts, seq_length)
    active = [(turn >= MAXR - token_counts)[None, :] for turn in range(MAXR)]
    inject = (
        jnp.einsum(
            "br,ref->bef",
            selected.astype(jnp.bfloat16),
            lax.all_gather(prelude_output, "dp", axis=0, tiled=True),
            preferred_element_type=jnp.float32,
        )
        .reshape(rows, local_width)
        .T
    )
    gain = norm_gain[:, None]
    gain_local = lax.dynamic_slice_in_dim(norm_gain, column_first, local_width, 0)[:, None]
    upstream = state_cotangent.reshape(rows, local_width).T.astype(jnp.float32)
    scaled = upstream * gain_local

    def project(state):
        return jnp.dot(core_weight, state, preferred_element_type=jnp.float32)

    states = [first_state]
    mixed_local, inverse_rms = [], []
    for turn in range(MAXR - 1):
        mixed = (project(states[turn]) + inject).astype(jnp.bfloat16)
        mixed_local.append(mixed.astype(jnp.float32))
        whole = spread(mixed, "mp", mp_count).reshape(full_width, rows).astype(jnp.float32)
        inverse = lax.rsqrt(jnp.sum(whole * whole, axis=0, keepdims=True) / full_width + EPS)
        inverse_rms.append(inverse)
        renewed = (gain * whole * inverse).astype(jnp.bfloat16)
        states.append(jnp.where(active[turn], renewed, states[turn]))

    product = project(states[2])
    last = (product + inject).astype(jnp.bfloat16).astype(jnp.float32)
    sums = jnp.stack(
        [
            jnp.sum(last * last, axis=0),
            jnp.sum(scaled * last, axis=0),
            jnp.sum(scaled * product, axis=0),
            jnp.sum(last * product, axis=0),
        ]
    )
    totals = jnp.sum(spread(sums, "mp", mp_count), axis=0)
    inverse_2 = lax.rsqrt(totals[0:1] / full_width + EPS)
    pull = inverse_2**3 * totals[1:2] / full_width
    delta_2 = jnp.where(active[2], inverse_2 * scaled - last * pull, 0.0).astype(jnp.bfloat16)

    inverse_1 = inverse_rms[1]
    inner_1 = (inverse_2 * totals[2:3] - pull * totals[3:4]) / inverse_1

    partial = lax.dot_general(
        core_weight, delta_2, (((0,), (0,)), ((), ())), preferred_element_type=jnp.float32
    ).astype(jnp.bfloat16)
    pieces = lax.all_to_all(partial.reshape(mp_count, local_width, rows), "mp", 0, 0)
    grad_in = jnp.sum(pieces.astype(jnp.float32), axis=0)
    delta_1 = jnp.where(
        active[1],
        inverse_1 * (grad_in * gain_local)
        - mixed_local[1] * (inverse_1**3 * inner_1 / full_width),
        0.0,
    ).astype(jnp.bfloat16)

    def outer(state, delta):
        return lax.dot_general(
            state, delta, (((1,), (1,)), ((), ())), preferred_element_type=jnp.float32
        )

    weight_grad = (outer(states[2], delta_2) + outer(states[1], delta_1)).astype(jnp.bfloat16)
    parts = lax.all_to_all(
        weight_grad.reshape(dp_count, full_width // dp_count, local_width), "dp", 0, 0
    )
    return jnp.sum(parts.astype(jnp.float32), axis=0).T


def solution(mesh):
    return jax.shard_map(
        local,
        mesh=mesh,
        in_specs=(
            P("dp", None, "mp"),
            P("dp", None, "mp"),
            P("mp", None),
            P(),
            P("dp", None, "mp"),
            P(),
            P(),
        ),
        out_specs=P("mp", "dp"),
        check_vma=False,
    )
```

time: 1000 us -> 421 us (0.42)
  the two profiles are of different devices: /device:TPU:192 before, /device:TPU:9 now
where the time goes in v1:
time: 421 us; the launch traced here: 420 us
  waiting for transfers between devices  175 us (42%)
  blocking collectives  129 us (31%)
  starting transfers between devices  63.8 us (15%)
  local copies, waits for them, and re-layouts  24.7 us (6%)
  other arithmetic  14.5 us (3%)
  matrix products  13.5 us (3%)
    all_to_all x4, waiting for transfers between devices, spread(): lax.all_to_all(jnp.broadcast_to(block[None], (count,) + block.shape), axi...  129 us
    all_gather x1, blocking collectives, local(): lax.all_gather(prelude_output, 'dp', axis=0, tiled=True)  70 us
    all_to_all x1, blocking collectives, local(): lax.all_to_all(weight_grad.reshape(dp_count, full_width // dp_count, loca...  58.8 us
    all_to_all x4, starting transfers between devices, spread(): lax.all_to_all(jnp.broadcast_to(block[None], (count,) + block.shape), axi...  53.7 us
    all_to_all x1, waiting for transfers between devices, local(): lax.all_to_all(partial.reshape(mp_count, local_width, rows), 'mp', 0, 0)  45.4 us
    all_to_all x1, starting transfers between devices, local(): lax.all_to_all(partial.reshape(mp_count, local_width, rows), 'mp', 0, 0)  10.1 us
    dot_general x2, matrix products, outer(): lax.dot_general(state, delta, (((1,), (1,)), ((), ())), preferred_element...  8.46 us
  transfers between devices with their start and end apart: 5, of which 4 were waited for; matrix products, arithmetic and copies ran while one was open for 1% of the time, Pallas kernels for 0%

profile of v1, /device:TPU:9, one launch (start us, length us, event | category | flops | bytes accessed | tf_op | source)
XLA Modules:
  0.0 420.4 jit_solution(297907198554677261)
XLA Ops:
  0.0 1.1 copy.29
  1.1 1.3 broadcast_in_dim.95
  2.4 19.9 %all-to-all-start = ((bf16[32,165,128]{2,1,0:T(8,128)(2,1)}), bf16[32,165,128]{2,1,0:T(8,128)(2,1)}, u32[]{:S(2)}, u32[]{:S(2)}) async-start(bf16[32,165,128]{2,1,0:T(8,128)(2,1)} %broadcast_in_dim.95), calls=%async_computation | async-start | bytes 2752512 | tf_op jit(solution)/shard_map/all_to_all | solution.py:11
  22.3 0.2 convert_reduce_fusion.2
  22.5 70.0 %all_gather.3 = bf16[72,32,165]{2,1,0:T(8,128)(2,1)S(1)} all-gather(bf16[3,32,165]{2,1,0:T(8,128)(2,1)S(1)} %copy-done.5), channel_id=1, replica_groups=mesh['dp'=24,'mp'=32] {'dp'}, dimensions={0}, use_global_device_ids=true | all-gather | bytes 792000 | tf_op jit(solution)/shard_map/all_gather | solution.py:43
  92.5 0.8 fusion.4
  93.3 0.1 copy.32
  93.5 1.5 reshape.104
  95.0 0.6 fusion.7
  95.7 1.3 broadcast_in_dim.96
  96.9 16.9 %all-to-all-start.1 = ((bf16[32,165,128]{2,1,0:T(8,128)(2,1)}), bf16[32,165,128]{2,1,0:T(8,128)(2,1)}, u32[]{:S(2)}, u32[]{:S(2)}) async-start(bf16[32,165,128]{2,1,0:T(8,128)(2,1)} %broadcast_in_dim.96), calls=%async_computation.1 | async-start | bytes 2752512 | tf_op jit(solution)/shard_map/all_to_all | solution.py:11
  113.9 0.1 select_reduce_fusion
  114.0 0.1 broadcast_in_dim.93
  114.1 0.1 le.47
  114.2 52.6 %all-to-all-done.1 = bf16[32,165,128]{2,1,0:T(8,128)(2,1)} async-done(((bf16[32,165,128]{2,1,0:T(8,128)(2,1)}), bf16[32,165,128]{2,1,0:T(8,128)(2,1)}, u32[]{:S(2)}, u32[]{:S(2)}) %all-to-all-start.1) | async-done | bytes 1351712 | tf_op jit(solution)/shard_map/all_to_all | solution.py:11
  166.8 2.1 multiply_reduce_fusion.1
  168.8 2.8 reshape.108
  171.7 3.8 fusion.2
  175.5 0.6 fusion.8
  176.1 1.3 broadcast_in_dim.97
  177.4 12.2 %all-to-all-start.2 = ((bf16[32,165,128]{2,1,0:T(8,128)(2,1)}), bf16[32,165,128]{2,1,0:T(8,128)(2,1)}, u32[]{:S(2)}, u32[]{:S(2)}) async-start(bf16[32,165,128]{2,1,0:T(8,128)(2,1)} %broadcast_in_dim.97), calls=%async_computation.2 | async-start | bytes 2752512 | tf_op jit(solution)/shard_map/all_to_all | solution.py:11
  189.6 0.1 dynamic_slice.3
  189.7 0.1 broadcast_in_dim.91
  189.7 0.1 le.44
  189.9 0.1 copy.33
  190.0 63.7 %all-to-all-done.2 = bf16[32,165,128]{2,1,0:T(8,128)(2,1)} async-done(((bf16[32,165,128]{2,1,0:T(8,128)(2,1)}), bf16[32,165,128]{2,1,0:T(8,128)(2,1)}, u32[]{:S(2)}, u32[]{:S(2)}) %all-to-all-start.2) | async-done | bytes 1351712 | tf_op jit(solution)/shard_map/all_to_all | solution.py:11
  253.7 2.1 multiply_reduce_fusion
  255.8 2.8 reshape.109
  258.6 3.6 fusion.3
  262.2 1.1 copy-done.1
  263.2 0.7 fusion.10
  263.9 0.6 broadcast_in_dim.100
  264.5 4.7 %all-to-all-start.3 = ((f32[32,4,128]{2,1,0:T(4,128)}), f32[32,4,128]{2,1,0:T(4,128)S(1)}, u32[]{:S(2)}, u32[]{:S(2)}) async-start(f32[32,4,128]{2,1,0:T(4,128)} %broadcast_in_dim.100), calls=%async_computation.3 | async-start | bytes 131072 | tf_op jit(solution)/shard_map/all_to_all | solution.py:11
  269.3 0.1 broadcast_in_dim.98
  269.4 0.1 le.50
  269.5 13.0 %all-to-all-done.3 = f32[32,4,128]{2,1,0:T(4,128)S(1)} async-done(((f32[32,4,128]{2,1,0:T(4,128)}), f32[32,4,128]{2,1,0:T(4,128)S(1)}, u32[]{:S(2)}, u32[]{:S(2)}) %all-to-all-start.3) | async-done | bytes 65568 | tf_op jit(solution)/shard_map/all_to_all | solution.py:11
  282.5 0.1 fusion.14
  282.6 2.3 fusion.1
  284.9 2.4 reshape.106
  287.3 10.1 %all-to-all-start.4 = ((bf16[32,165,128]{2,1,0:T(8,128)(2,1)}), bf16[32,165,128]{2,1,0:T(8,128)(2,1)}, u32[]{:S(2)}, u32[]{:S(2)}) async-start(bf16[32,165,128]{2,1,0:T(8,128)(2,1)} %reshape.106), calls=%async_computation.4 | async-start | bytes 2752512 | tf_op jit(solution)/shard_map/all_to_all | solution.py:89
  297.4 4.2 fusion.36
  301.6 45.4 %all-to-all-done.4 = bf16[32,165,128]{2,1,0:T(8,128)(2,1)} async-done(((bf16[32,165,128]{2,1,0:T(8,128)(2,1)}), bf16[32,165,128]{2,1,0:T(8,128)(2,1)}, u32[]{:S(2)}, u32[]{:S(2)}) %all-to-all-start.4) | async-done | bytes 1351712 | tf_op jit(solution)/shard_map/all_to_all | solution.py:89
  346.9 1.5 convert_reduce_fusion.1
  348.5 4.3 %fusion = bf16[5280,165]{0,1:T(8,128)(2,1)} fusion(f32[5280,165]{0,1:T(8,128)} %fusion.36, bf16[5280,128]{1,0:T(8,128)(2,1)S(1)} %fusion.2, bf16[165,128]{1,0:T(8,128)(2,1)S(1)} %fusion.8, f32[165,128]{1,0:T(8,128)S(1)} %convert_reduce_fusion.1, f32[128]{0:T(128)S(1)} %get-tuple-element.10, f32[165]{0:T(256)S(1)} %dynamic_slice.3, f32[128]{0:T(128)S(1)} %fusion.31, ...), kind=kOutput, calls=%fused_computation.1 | convolution fusion | flops 224917440 | bytes 6707412 | tf_op jit(solution)/shard_map/dot_general | solution.py:99
  352.8 5.8 %reshape.107 = bf16[24,220,165]{1,0,2:T(8,128)(2,1)} reshape(bf16[5280,165]{0,1:T(8,128)(2,1)} %fusion) | data formatting | bytes 3484800 | tf_op jit(solution)/shard_map/reshape | solution.py:105
  358.6 2.0 copy.35
  360.6 58.8 %all_to_all.30 = bf16[24,220,165]{1,2,0:T(8,128)(2,1)S(1)} all-to-all(bf16[24,220,165]{1,2,0:T(8,128)(2,1)S(1)} %copy.35), channel_id=1, replica_groups=mesh['dp'=24,'mp'=32] {'dp'}, dimensions={0} | all-to-all | bytes 3484800 | tf_op jit(solution)/shard_map/all_to_all | solution.py:104
  419.4 1.0 convert_reduce_fusion
  (25 shorter events, 0.2 us)
Async XLA Ops:
  0.0 95.0 %copy-start = (bf16[165,5280]{1,0:T(8,128)(2,1)S(1)}, bf16[165,5280]{1,0:T(8,128)(2,1)}, u32[]{:S(2)}) copy-start(bf16[165,5280]{1,0:T(8,128)(2,1)} %param.9) | copy-start | bytes 5227204
  1.1 21.2 %copy-start.7 = (s32[72]{0:T(128)S(1)}, s32[72]{0:T(128)}, u32[]{:S(2)}) copy-start(s32[72]{0:T(128)} %param.13) | copy-start | bytes 868
  1.1 21.4 %copy-start.5 = (bf16[3,32,165]{2,1,0:T(8,128)(2,1)S(1)}, bf16[3,32,165]{2,1,0:T(8,128)(2,1)}, u32[]{:S(2)}) copy-start(bf16[3,32,165]{2,1,0:T(8,128)(2,1)} %param.7) | copy-start | bytes 95044
  2.4 91.0 %all-to-all-start = ((bf16[32,165,128]{2,1,0:T(8,128)(2,1)}), bf16[32,165,128]{2,1,0:T(8,128)(2,1)}, u32[]{:S(2)}, u32[]{:S(2)}) async-start(bf16[32,165,128]{2,1,0:T(8,128)(2,1)} %broadcast_in_dim.95), calls=%async_computation | async-start | bytes 2752512 | tf_op jit(solution)/shard_map/all_to_all | solution.py:11
  95.0 1.9 copy-start.2
  95.7 18.2 %copy-start.6 = (s32[72]{0:T(128)S(1)}, s32[72]{0:T(128)}, u32[]{:S(2)}) copy-start(s32[72]{0:T(128)} %param.12) | copy-start | bytes 868
  96.9 69.8 %all-to-all-start.1 = ((bf16[32,165,128]{2,1,0:T(8,128)(2,1)}), bf16[32,165,128]{2,1,0:T(8,128)(2,1)}, u32[]{:S(2)}, u32[]{:S(2)}) async-start(bf16[32,165,128]{2,1,0:T(8,128)(2,1)} %broadcast_in_dim.96), calls=%async_computation.1 | async-start | bytes 2752512 | tf_op jit(solution)/shard_map/all_to_all | solution.py:11
  168.8 2.8 copy-start.3
  176.1 13.7 %copy-start.4 = (bf16[4,32,165]{2,1,0:T(8,128)(2,1)S(1)}, bf16[4,32,165]{2,1,0:T(8,128)(2,1)}, u32[]{:S(2)}) copy-start(bf16[4,32,165]{2,1,0:T(8,128)(2,1)} %param.11) | copy-start | bytes 126724
  177.4 76.3 %all-to-all-start.2 = ((bf16[32,165,128]{2,1,0:T(8,128)(2,1)}), bf16[32,165,128]{2,1,0:T(8,128)(2,1)}, u32[]{:S(2)}, u32[]{:S(2)}) async-start(bf16[32,165,128]{2,1,0:T(8,128)(2,1)} %broadcast_in_dim.97), calls=%async_computation.2 | async-start | bytes 2752512 | tf_op jit(solution)/shard_map/all_to_all | solution.py:11
  262.1 1.1 copy-start.1
  264.5 17.9 %all-to-all-start.3 = ((f32[32,4,128]{2,1,0:T(4,128)}), f32[32,4,128]{2,1,0:T(4,128)S(1)}, u32[]{:S(2)}, u32[]{:S(2)}) async-start(f32[32,4,128]{2,1,0:T(4,128)} %broadcast_in_dim.100), calls=%async_computation.3 | async-start | bytes 131072 | tf_op jit(solution)/shard_map/all_to_all | solution.py:11
  287.3 59.7 %all-to-all-start.4 = ((bf16[32,165,128]{2,1,0:T(8,128)(2,1)}), bf16[32,165,128]{2,1,0:T(8,128)(2,1)}, u32[]{:S(2)}, u32[]{:S(2)}) async-start(bf16[32,165,128]{2,1,0:T(8,128)(2,1)} %reshape.106), calls=%async_computation.4 | async-start | bytes 2752512 | tf_op jit(solution)/shard_map/all_to_all | solution.py:89
